TPU v7x, 512 devices: a whole 4x4x16 slice. The times are simulated.
512 devices in a mesh: gx: 64 (over z, y), gz: 8 (over x, core).
Axes of the slice: x: 4, y: 4, z: 16, core: 2. Of those that a mesh axis runs over, the one named last changes fastest.
Arguments:
- tokens: bfloat16 [4, 256, 64, 768], P(None, 'gx', 'gz'), may hold values from -60 to 60
- cross_qkv: bfloat16 [768, 2304], P(None, 'gx'), may hold values from -16 to 16
- cross_out: bfloat16 [768, 768], P('gx'), may hold values from -0.21875 to 0.21875
- depth_qkv: bfloat16 [768, 2304], P(None, 'gx'), may hold values from -16 to 16
- depth_out: bfloat16 [768, 768], P('gx'), may hold values from -0.21875 to 0.21875
- up_proj: bfloat16 [768, 3072], P(None, 'gz'), may hold values from -0.21875 to 0.21875
- down_proj: bfloat16 [3072, 768], P('gz'), may hold values from -0.109375 to 0.109375
- gains: float32 [3, 768], replicated, may hold values from 0.5 to 1.5
- head_weight: float32 [768], replicated, may hold values from -0.21875 to 0.21875
- head_bias: float32 [1], replicated, may hold values from -1 to 1
Outputs:
- features: bfloat16 [4, 256, 64, 768], P(None, 'gx', 'gz')
- geotime: float32 [4, 256, 64], P(None, 'gx', 'gz')
All inputs are finite; a program needn't handle non-finite values.
Results may differ from a plain program's by a relative error of at most 0.013.
Values may be sent and summed in bfloat16 or wider, within the bound.
A program may use at most 64 MiB of HBM per device.

v0:
```python
import math
import jax
import jax.numpy as jnp
from jax import lax
from jax.sharding import PartitionSpec as P

HDIM = 64
log_span = math.log(256.0)


def carried_in(shard, axis, combine, identity):
    peers, position = (lax.axis_size(axis), lax.axis_index(axis))
    everything = lax.all_gather(shard, axis)
    start = jnp.broadcast_to(jnp.asarray(identity, shard.dtype), shard.shape)

    def step(k, before):
        reached = k < position
        new = combine(before, everything[k])
        return jnp.where(reached, new, before)

    return lax.fori_loop(0, peers, step, start)


def encodings(inlines, crosslines, depths, cross_start, depth_start, model_width):
    pairs = model_width // 2
    index = jnp.arange(pairs)
    freq = math.pi * jnp.exp(-log_span * index.astype(jnp.float32) / pairs)
    which = index % 3
    inline_pos = jnp.arange(inlines).astype(jnp.float32)[:, None, None, None]
    cross_pos = (cross_start + jnp.arange(crosslines)).astype(jnp.float32)[None, :, None, None]
    depth_pos = (depth_start + jnp.arange(depths)).astype(jnp.float32)[None, None, :, None]
    zeros = jnp.zeros((inlines, crosslines, depths, pairs), jnp.float32)
    position = jnp.where(
        which == 0, inline_pos + zeros, jnp.where(which == 1, cross_pos + zeros, depth_pos + zeros)
    )
    angle = position * freq
    return jnp.stack([jnp.sin(angle), jnp.cos(angle)], -1).reshape(
        inlines, crosslines, depths, model_width
    )


def normalize(stream, gain):
    scale = lax.rsqrt(jnp.mean(stream * stream, -1, keepdims=True) + 1e-05)
    return (stream * scale * gain).astype(jnp.bfloat16)


def attend(queries, keys, values):
    scale = queries.shape[-1] ** (-0.5)
    scores = (
        jnp.einsum("...qe,...ke->...qk", queries, keys, preferred_element_type=jnp.float32) * scale
    )
    scores = scores - jnp.max(scores, -1, keepdims=True)
    expo = jnp.exp(scores)
    weights = (expo / jnp.sum(expo, -1, keepdims=True)).astype(jnp.bfloat16)
    mixed = jnp.einsum("...qk,...ke->...qe", weights, values, preferred_element_type=jnp.float32)
    return mixed.astype(jnp.bfloat16)


def attend_items(trio):
    return attend(trio[0], trio[1], trio[2])


def body(
    tokens,
    cross_qkv,
    cross_out,
    depth_qkv,
    depth_out,
    up_proj,
    down_proj,
    gains,
    head_weight,
    head_bias,
):
    inlines, cross_dev, depth_dev, model_width = tokens.shape
    tok_rows = inlines * cross_dev * depth_dev
    head_count = model_width // HDIM
    cross_group = lax.axis_size("gx")
    encoding = encodings(
        inlines,
        cross_dev,
        depth_dev,
        lax.axis_index("gx") * cross_dev,
        lax.axis_index("gz") * depth_dev,
        model_width,
    )
    stream = (tokens.astype(jnp.float32) + encoding).reshape(tok_rows, model_width)
    normed = normalize(stream, gains[0])
    packed = jnp.dot(
        normed,
        lax.all_gather(cross_qkv, "gx", axis=1, tiled=True),
        preferred_element_type=jnp.float32,
    ).astype(jnp.bfloat16)
    packed = packed.reshape(inlines, cross_dev, depth_dev, 3, head_count, HDIM)
    lined = jnp.transpose(packed, (3, 0, 2, 4, 1, 5))
    per_item = inlines * depth_dev * head_count // cross_group
    lined = lined.reshape(3, cross_group, per_item, cross_dev, HDIM)
    mixed = attend_items(
        (
            lax.all_to_all(lined[0], "gx", split_axis=0, concat_axis=2, tiled=True),
            lax.all_to_all(lined[1], "gx", split_axis=0, concat_axis=2, tiled=True),
            lax.all_to_all(lined[2], "gx", split_axis=0, concat_axis=2, tiled=True),
        )
    )
    mixed = lax.all_to_all(mixed, "gx", split_axis=2, concat_axis=0, tiled=True)
    mixed = jnp.transpose(
        mixed.reshape(inlines, depth_dev, head_count, cross_dev, HDIM), (0, 3, 1, 2, 4)
    ).reshape(tok_rows, model_width)
    columns = mixed
    stream = stream + jnp.dot(
        columns,
        lax.all_gather(cross_out, "gx", axis=0, tiled=True),
        preferred_element_type=jnp.float32,
    )
    normed = normalize(stream, gains[1])
    packed = jnp.dot(
        normed,
        lax.all_gather(depth_qkv, "gx", axis=1, tiled=True),
        preferred_element_type=jnp.float32,
    ).astype(jnp.bfloat16)
    packed = packed.reshape(inlines, cross_dev, depth_dev, 3, head_count, HDIM)
    lined = jnp.transpose(packed, (3, 0, 1, 4, 2, 5))
    all_keys, all_values = (
        lax.all_gather(lined[1], "gz", axis=3, tiled=True),
        lax.all_gather(lined[2], "gz", axis=3, tiled=True),
    )
    mixed = attend(lined[0], all_keys, all_values)
    mixed = jnp.transpose(mixed, (0, 1, 3, 2, 4)).reshape(tok_rows, model_width)
    columns = mixed
    stream = stream + jnp.dot(
        columns,
        lax.all_gather(depth_out, "gx", axis=0, tiled=True),
        preferred_element_type=jnp.float32,
    )
    normed = normalize(stream, gains[2])
    hidden = jax.nn.gelu(
        jnp.dot(
            lax.all_gather(normed, "gz", axis=0, tiled=True),
            up_proj,
            preferred_element_type=jnp.float32,
        )
    ).astype(jnp.bfloat16)
    stream = stream + lax.psum_scatter(
        jnp.dot(hidden, down_proj, preferred_element_type=jnp.float32).astype(jnp.bfloat16),
        "gz",
        scatter_dimension=0,
        tiled=True,
    ).astype(jnp.float32)
    features = stream.astype(jnp.bfloat16).reshape(inlines, cross_dev, depth_dev, model_width)
    thickness = jax.nn.softplus(
        jnp.dot(stream, head_weight, precision=lax.Precision.HIGHEST) + head_bias[0]
    )
    local_time = jnp.cumsum(thickness.reshape(inlines, cross_dev, depth_dev), axis=2)
    line_total = local_time[:, :, -1]
    carried = carried_in(
        line_total, "gz", lambda earlier, later: earlier + later, jnp.zeros_like(line_total)
    )
    geotime = local_time + carried[:, :, None]
    return (features, geotime)


def solution(mesh):
    return jax.shard_map(
        body,
        mesh=mesh,
        in_specs=(
            P(None, "gx", "gz", None),
            P(None, "gx"),
            P("gx", None),
            P(None, "gx"),
            P("gx", None),
            P(None, "gz"),
            P("gz", None),
            P(),
            P(),
            P(),
        ),
        out_specs=(P(None, "gx", "gz", None), P(None, "gx", "gz")),
        check_vma=False,
    )
```

profile of v0, /device:TPU:1, one launch (start us, length us, event | category | flops | bytes accessed | tf_op | source)
XLA Modules:
  0.0 772.2 jit_solution(6534772506447443359)
XLA Ops:
  7.2 0.7 all-gather.21.cloned.1.call-update
  8.0 0.7 all-gather.23.cloned.1.call-update
  8.7 0.7 all-gather.25.cloned.1.call-update
  9.5 0.8 fusion.41
  10.3 6.4 copy.57
  16.6 4.4 copy.58
  21.4 132.3 %all-gather.21.cloned.1.call-done = bf16[64,36,768]{2,1,0:T(8,128)(2,1)} async-done(((bf16[1,36,768]{2,1,0:T(8,128)(2,1)}), bf16[64,36,768]{2,1,0:T(8,128)(2,1)}) %all-gather.21.cloned.1.call-update) | async-done | bytes 3538960 | tf_op jit(solution)/shard_map/all_gather | solution.py:91
  153.7 6.2 reshape.159
  159.8 3.3 convolution_convert_fusion.1
  163.1 1.0 reshape.145
  164.1 1.1 fusion.53
  165.6 0.9 reshape.175
  166.5 8.7 %all-to-all-start.1 = ((bf16[64,2,768]{2,1,0:T(2,128)(2,1)}), bf16[64,2,768]{2,1,0:T(2,128)(2,1)S(1)}, u32[]{:S(2)}, u32[]{:S(2)}) async-start(bf16[64,2,768]{2,1,0:T(2,128)(2,1)} %reshape.175), calls=%async_computation.1 | async-start | bytes 393216 | tf_op jit(solution)/shard_map/all_to_all | solution.py:101
  175.5 0.9 reshape.173
  176.5 15.4 %all-to-all-done.1 = bf16[64,2,768]{2,1,0:T(2,128)(2,1)S(1)} async-done(((bf16[64,2,768]{2,1,0:T(2,128)(2,1)}), bf16[64,2,768]{2,1,0:T(2,128)(2,1)S(1)}, u32[]{:S(2)}, u32[]{:S(2)}) %all-to-all-start.1) | async-done | bytes 196640 | tf_op jit(solution)/shard_map/all_to_all | solution.py:101
  191.9 4.6 all-to-all-start
  196.8 0.9 reshape.171
  197.7 15.1 %all-to-all-done = bf16[64,2,768]{2,1,0:T(2,128)(2,1)S(1)} async-done(((bf16[64,2,768]{2,1,0:T(2,128)(2,1)}), bf16[64,2,768]{2,1,0:T(2,128)(2,1)S(1)}, u32[]{:S(2)}, u32[]{:S(2)}) %all-to-all-start) | async-done | bytes 196640 | tf_op jit(solution)/shard_map/all_to_all | solution.py:100
  212.9 4.6 all-to-all-start.2
  218.9 15.0 %all-to-all-done.2 = bf16[64,2,768]{2,1,0:T(2,128)(2,1)S(1)} async-done(((bf16[64,2,768]{2,1,0:T(2,128)(2,1)}), bf16[64,2,768]{2,1,0:T(2,128)(2,1)S(1)}, u32[]{:S(2)}, u32[]{:S(2)}) %all-to-all-start.2) | async-done | bytes 196640 | tf_op jit(solution)/shard_map/all_to_all | solution.py:102
  234.4 1.8 fusion.55
  236.2 1.7 fusion.27
  238.2 1.0 reshape.177
  239.2 4.6 all-to-all-start.3
  244.1 49.5 %all-gather.23.cloned.1.call-done = bf16[64,12,768]{2,1,0:T(8,128)(2,1)} async-done(((bf16[1,12,768]{2,1,0:T(8,128)(2,1)}), bf16[64,12,768]{2,1,0:T(8,128)(2,1)}) %all-gather.23.cloned.1.call-update) | async-done | bytes 1179664 | tf_op jit(solution)/shard_map/all_gather | solution.py:112
  293.6 2.2 reshape.161
  295.9 142.8 %all-gather.25.cloned.1.call-done = bf16[64,36,768]{2,1,0:T(8,128)(2,1)} async-done(((bf16[1,36,768]{2,1,0:T(8,128)(2,1)}), bf16[64,36,768]{2,1,0:T(8,128)(2,1)}) %all-gather.25.cloned.1.call-update) | async-done | bytes 3538960 | tf_op jit(solution)/shard_map/all_gather | solution.py:118
  438.7 6.2 reshape.163
  446.2 0.7 copy-done.1
  447.0 3.3 convolution_convert_fusion
  450.3 1.0 reshape.151
  451.6 1.0 fusion.54
  453.2 122.6 %all-gather.27.cloned.1.call-done = bf16[64,12,768]{2,1,0:T(8,128)(2,1)} async-done(((bf16[1,12,768]{2,1,0:T(8,128)(2,1)}), bf16[64,12,768]{2,1,0:T(8,128)(2,1)}) %all-gather.27.cloned.1.call-update) | async-done | bytes 1179664 | tf_op jit(solution)/shard_map/all_gather | solution.py:132
  575.8 2.2 reshape.165
  578.1 44.5 %all-gather.17.cloned.1.call-done = bf16[1,4,4,12,64,64]{5,4,3,2,1,0:T(8,128)(2,1)} async-done(((bf16[1,4,4,12,8,64]{5,4,3,2,1,0:T(8,128)(2,1)}), bf16[1,4,4,12,64,64]{5,4,3,2,1,0:T(8,128)(2,1)}) %all-gather.17.cloned.1.call-update) | async-done | bytes 1572880 | tf_op jit(solution)/shard_map/all_gather | solution.py:124
  622.5 4.6 fusion.56
  627.2 37.7 %all-gather.19.cloned.1.call-done = bf16[1,4,4,12,64,64]{5,4,3,2,1,0:T(8,128)(2,1)} async-done(((bf16[1,4,4,12,8,64]{5,4,3,2,1,0:T(8,128)(2,1)}), bf16[1,4,4,12,64,64]{5,4,3,2,1,0:T(8,128)(2,1)}) %all-gather.19.cloned.1.call-update) | async-done | bytes 1572880 | tf_op jit(solution)/shard_map/all_gather | solution.py:125
  664.9 3.1 fusion.24
  669.5 0.8 multiply_convert_fusion
  670.3 33.1 %all-gather.15.cloned.1.call-done = bf16[1024,768]{1,0:T(8,128)(2,1)} async-done(((bf16[128,768]{1,0:T(8,128)(2,1)}), bf16[1024,768]{1,0:T(8,128)(2,1)}) %all-gather.15.cloned.1.call-update) | async-done | bytes 1572880 | tf_op jit(solution)/shard_map/all_gather | solution.py:138
  703.5 4.6 convolution_convert_fusion.2
  708.2 0.7 copy-done.6
  709.5 37.5 %reduce-scatter.2.cloned.1.call-done = bf16[128,768]{1,0:T(8,128)(2,1)} async-done(((bf16[1024,768]{1,0:T(8,128)(2,1)}), bf16[128,768]{1,0:T(8,128)(2,1)}) %reduce-scatter.2.cloned.1.call-update) | async-done | bytes 196624 | tf_op jit(solution)/shard_map/reduce_scatter | solution.py:143
  747.0 1.4 compare_select_fusion
  748.4 0.7 reduce_window_sum.11
  749.3 13.5 %all-gather.2 = f32[32,4,1]{1,2,0:T(1,128)S(1)} all-gather(f32[4,4,1]{1,2,0:T(1,128)S(1)} %copy.75), channel_id=4, replica_groups=mesh['gx'=64,'gz'=8] {'gz'}, dimensions={0}, use_global_device_ids=true | all-gather | bytes 576 | tf_op jit(solution)/shard_map/all_gather | solution.py:13
  763.1 0.7 broadcast_add_fusion
  763.8 1.6 fusion.37
  (72 shorter events, 8.2 us)
Async XLA Ops:
  7.2 696.3 %copy-start = (bf16[384,768]{1,0:T(8,128)(2,1)S(1)}, bf16[384,768]{1,0:T(8,128)(2,1)}, u32[]{:S(2)}) copy-start(bf16[384,768]{1,0:T(8,128)(2,1)} %param.18) | copy-start | bytes 1769476
  7.2 146.5 %all-gather.21.cloned.1.call-start = ((), (), s32[]{:S(2)}) async-start(), calls=%async_computation.9 | async-start | bytes 3993600 | tf_op jit(solution)/shard_map/all_gather | solution.py:91
  7.9 285.7 %all-gather.23.cloned.1.call-start = ((), (), s32[]{:S(2)}) async-start(), calls=%async_computation.10 | async-start | bytes 1597440 | tf_op jit(solution)/shard_map/all_gather | solution.py:112
  8.7 430.0 %all-gather.25.cloned.1.call-start = ((), (), s32[]{:S(2)}) async-start(), calls=%async_computation.11 | async-start | bytes 3993600 | tf_op jit(solution)/shard_map/all_gather | solution.py:118
  16.6 4.4 copy-start.4
  16.6 4.6 copy-start.5
  165.2 10.0 %copy-start.3 = (bf16[1,4,8,12,4,64]{5,3,0,2,4,1:T(8,128)(2,1)S(1)}, bf16[1,4,8,12,4,64]{5,3,0,2,4,1:T(8,128)(2,1)}, u32[]{:S(2)}) copy-start(bf16[1,4,8,12,4,64]{5,3,0,2,4,1:T(8,128)(2,1)} %get-tuple-element.128) | copy-start | bytes 589828
  166.5 25.4 %all-to-all-start.1 = ((bf16[64,2,768]{2,1,0:T(2,128)(2,1)}), bf16[64,2,768]{2,1,0:T(2,128)(2,1)S(1)}, u32[]{:S(2)}, u32[]{:S(2)}) async-start(bf16[64,2,768]{2,1,0:T(2,128)(2,1)} %reshape.175), calls=%async_computation.1 | async-start | bytes 393216 | tf_op jit(solution)/shard_map/all_to_all | solution.py:101
  191.9 21.0 %all-to-all-start = ((bf16[64,2,768]{2,1,0:T(2,128)(2,1)}), bf16[64,2,768]{2,1,0:T(2,128)(2,1)S(1)}, u32[]{:S(2)}, u32[]{:S(2)}) async-start(bf16[64,2,768]{2,1,0:T(2,128)(2,1)} %reshape.173), calls=%async_computation | async-start | bytes 393216 | tf_op jit(solution)/shard_map/all_to_all | solution.py:100
  212.9 21.1 %all-to-all-start.2 = ((bf16[64,2,768]{2,1,0:T(2,128)(2,1)}), bf16[64,2,768]{2,1,0:T(2,128)(2,1)S(1)}, u32[]{:S(2)}, u32[]{:S(2)}) async-start(bf16[64,2,768]{2,1,0:T(2,128)(2,1)} %reshape.171), calls=%async_computation.2 | async-start | bytes 393216 | tf_op jit(solution)/shard_map/all_to_all | solution.py:102
  217.5 358.3 %all-gather.27.cloned.1.call-start = ((), (), s32[]{:S(2)}) async-start(), calls=%async_computation.12 | async-start | bytes 1597440 | tf_op jit(solution)/shard_map/all_gather | solution.py:132
  239.2 205.6 %all-to-all-start.3 = ((bf16[64,2,768]{2,1,0:T(2,128)(2,1)}), bf16[64,2,768]{2,1,0:T(2,128)(2,1)S(1)}, u32[]{:S(2)}, u32[]{:S(2)}) async-start(bf16[64,2,768]{2,1,0:T(2,128)(2,1)} %reshape.177), calls=%async_computation.3 | async-start | bytes 393216 | tf_op jit(solution)/shard_map/all_to_all | solution.py:105
  243.9 378.7 %all-gather.17.cloned.1.call-start = ((), (), s32[]{:S(2)}) async-start(), calls=%async_computation.7 | async-start | bytes 3538944 | tf_op jit(solution)/shard_map/all_gather | solution.py:124
  446.2 0.7 copy-start.1
  452.6 212.3 %all-gather.19.cloned.1.call-start = ((), (), s32[]{:S(2)}) async-start(), calls=%async_computation.8 | async-start | bytes 3538944 | tf_op jit(solution)/shard_map/all_gather | solution.py:125
  453.2 250.3 %all-gather.15.cloned.1.call-start = ((), (), s32[]{:S(2)}) async-start(), calls=%async_computation.5 | async-start | bytes 1769472 | tf_op jit(solution)/shard_map/all_gather | solution.py:138
  668.0 1.0 copy-start.2
  670.3 76.7 %reduce-scatter.2.cloned.1.call-start = ((), (), s32[]{:S(2)}) async-start(), calls=%async_computation.6 | async-start | bytes 1769472 | tf_op jit(solution)/shard_map/reduce_scatter | solution.py:143
  708.1 0.7 copy-start.6
Sparse Core Ops, SparseCore 0:
  11.0 142.6 all-gather.20
  156.6 136.9 all-gather.22
  296.6 142.0 all-gather.24
  441.5 134.2 all-gather.26
  577.8 44.7 all-gather.16
  624.5 40.3 all-gather.18
  670.4 33.0 all-gather.14
  708.3 38.6 reduce-scatter.1
where the time goes:
time: 773 us; the launch traced here: 772 us
  waiting for transfers between devices  649 us (84%)
  local copies, waits for them, and re-layouts  41.9 us (5%)
  matrix products  24.7 us (3%)
  starting transfers between devices  23.1 us (3%)
  between operations  15.2 us (2%)
  blocking collectives  13.5 us (2%)
    all_gather x1, waiting for transfers between devices, body(): lax.all_gather(depth_qkv, 'gx', axis=1, tiled=True)  143 us
    all_gather x1, waiting for transfers between devices, body(): lax.all_gather(cross_qkv, 'gx', axis=1, tiled=True)  132 us
    all_gather x1, waiting for transfers between devices, body(): lax.all_gather(depth_out, 'gx', axis=0, tiled=True)  123 us
    all_gather x1, waiting for transfers between devices, body(): lax.all_gather(cross_out, 'gx', axis=0, tiled=True)  49.5 us
    all_gather x1, waiting for transfers between devices, body(): lax.all_gather(lined[1], 'gz', axis=3, tiled=True)  44.5 us
    all_gather x1, waiting for transfers between devices, body(): lax.all_gather(lined[2], 'gz', axis=3, tiled=True)  37.7 us
    reduce_scatter x1, waiting for transfers between devices, body(): lax.psum_scatter(jnp.dot(hidden, down_proj, preferred_element_type=jnp.fl...  37.5 us
    all_gather x1, waiting for transfers between devices, body(): lax.all_gather(normed, 'gz', axis=0, tiled=True)  33.1 us
  transfers between devices with their start and end apart: 12, of which 11 were waited for; matrix products, arithmetic and copies ran while one was open for 7% of the time, Pallas kernels for 0%

commit v1 on v0

--- a/solution.py
+++ b/solution.py
@@ -99,7 +99,12 @@
         (
             lax.all_to_all(lined[0], "gx", split_axis=0, concat_axis=2, tiled=True),
             lax.all_to_all(lined[1], "gx", split_axis=0, concat_axis=2, tiled=True),
-            lax.all_to_all(lined[2], "gx", split_axis=0, concat_axis=2, tiled=True),
+            jnp.concatenate(
+                lax.all_to_all(
+                    jnp.stack(jnp.split(lined[2], lax.axis_size("gx"), axis=0)), "gx", 0, 0
+                ),
+                axis=2,
+            ),
         )
     )
     mixed = lax.all_to_all(mixed, "gx", split_axis=2, concat_axis=0, tiled=True)

time: 773 us -> 773 us (level)
    unnamed x27 -> x90, local copies, waits for them, and re-layouts: 23.7 us -> 24.5 us
where the time goes in v1:
time: 773 us; the launch traced here: 772 us
  waiting for transfers between devices  648 us (84%)
  local copies, waits for them, and re-layouts  42.6 us (6%)
  matrix products  24.7 us (3%)
  starting transfers between devices  23.1 us (3%)
  between operations  15.4 us (2%)
  blocking collectives  13.4 us (2%)
    all_gather x1, waiting for transfers between devices, body(): lax.all_gather(depth_qkv, 'gx', axis=1, tiled=True)  143 us
    all_gather x1, waiting for transfers between devices, body(): lax.all_gather(cross_qkv, 'gx', axis=1, tiled=True)  132 us
    all_gather x1, waiting for transfers between devices, body(): lax.all_gather(depth_out, 'gx', axis=0, tiled=True)  123 us
    all_gather x1, waiting for transfers between devices, body(): lax.all_gather(cross_out, 'gx', axis=0, tiled=True)  48.2 us
    all_gather x1, waiting for transfers between devices, body(): lax.all_gather(lined[1], 'gz', axis=3, tiled=True)  44.5 us
    all_gather x1, waiting for transfers between devices, body(): lax.all_gather(lined[2], 'gz', axis=3, tiled=True)  37.7 us
    reduce_scatter x1, waiting for transfers between devices, body(): lax.psum_scatter(jnp.dot(hidden, down_proj, preferred_element_type=jnp.fl...  37.5 us
    all_gather x1, waiting for transfers between devices, body(): lax.all_gather(normed, 'gz', axis=0, tiled=True)  33.1 us
  transfers between devices with their start and end apart: 12, of which 11 were waited for; matrix products, arithmetic and copies ran while one was open for 7% of the time, Pallas kernels for 0%

profile of v1, /device:TPU:1, one launch (start us, length us, event | category | flops | bytes accessed | tf_op | source)
XLA Modules:
  0.0 772.0 jit_solution(13893064907834304056)
XLA Ops:
  7.2 0.7 all-gather.21.cloned.1.call-update
  8.0 0.7 all-gather.23.cloned.1.call-update
  8.7 0.7 all-gather.25.cloned.1.call-update
  9.5 0.8 fusion.41
  10.3 6.4 copy.120
  16.6 4.4 copy.121
  21.4 132.3 %all-gather.21.cloned.1.call-done = bf16[64,36,768]{2,1,0:T(8,128)(2,1)} async-done(((bf16[1,36,768]{2,1,0:T(8,128)(2,1)}), bf16[64,36,768]{2,1,0:T(8,128)(2,1)}) %all-gather.21.cloned.1.call-update) | async-done | bytes 3538960 | tf_op jit(solution)/shard_map/all_gather | solution.py:91
  153.7 6.2 reshape.164
  159.8 3.3 convolution_convert_fusion.1
  163.1 1.0 reshape.149
  164.1 1.1 fusion.53
  166.6 0.9 reshape.176
  167.5 8.7 %all-to-all-start.2 = ((bf16[64,2,768]{2,1,0:T(2,128)(2,1)}), bf16[64,2,768]{2,1,0:T(2,128)(2,1)S(1)}, u32[]{:S(2)}, u32[]{:S(2)}) async-start(bf16[64,2,768]{2,1,0:T(2,128)(2,1)} %reshape.176), calls=%async_computation.2 | async-start | bytes 393216 | tf_op jit(solution)/shard_map/all_to_all | solution.py:103
  176.5 0.9 reshape.180
  177.5 15.4 %all-to-all-done.2 = bf16[64,2,768]{2,1,0:T(2,128)(2,1)S(1)} async-done(((bf16[64,2,768]{2,1,0:T(2,128)(2,1)}), bf16[64,2,768]{2,1,0:T(2,128)(2,1)S(1)}, u32[]{:S(2)}, u32[]{:S(2)}) %all-to-all-start.2) | async-done | bytes 196640 | tf_op jit(solution)/shard_map/all_to_all | solution.py:103
  192.9 4.6 all-to-all-start.1
  197.8 0.9 reshape.178
  198.8 15.3 %all-to-all-done.1 = bf16[64,2,768]{2,1,0:T(2,128)(2,1)S(1)} async-done(((bf16[64,2,768]{2,1,0:T(2,128)(2,1)}), bf16[64,2,768]{2,1,0:T(2,128)(2,1)S(1)}, u32[]{:S(2)}, u32[]{:S(2)}) %all-to-all-start.1) | async-done | bytes 196640 | tf_op jit(solution)/shard_map/all_to_all | solution.py:101
  214.1 4.6 all-to-all-start
  220.1 15.1 %all-to-all-done = bf16[64,2,768]{2,1,0:T(2,128)(2,1)S(1)} async-done(((bf16[64,2,768]{2,1,0:T(2,128)(2,1)}), bf16[64,2,768]{2,1,0:T(2,128)(2,1)S(1)}, u32[]{:S(2)}, u32[]{:S(2)}) %all-to-all-start) | async-done | bytes 196640 | tf_op jit(solution)/shard_map/all_to_all | solution.py:100
  235.7 1.8 fusion.55
  237.5 1.7 fusion.27
  239.5 1.0 reshape.182
  240.5 4.8 all-to-all-start.3
  245.4 48.2 %all-gather.23.cloned.1.call-done = bf16[64,12,768]{2,1,0:T(8,128)(2,1)} async-done(((bf16[1,12,768]{2,1,0:T(8,128)(2,1)}), bf16[64,12,768]{2,1,0:T(8,128)(2,1)}) %all-gather.23.cloned.1.call-update) | async-done | bytes 1179664 | tf_op jit(solution)/shard_map/all_gather | solution.py:117
  293.5 2.2 reshape.166
  295.8 142.7 %all-gather.25.cloned.1.call-done = bf16[64,36,768]{2,1,0:T(8,128)(2,1)} async-done(((bf16[1,36,768]{2,1,0:T(8,128)(2,1)}), bf16[64,36,768]{2,1,0:T(8,128)(2,1)}) %all-gather.25.cloned.1.call-update) | async-done | bytes 3538960 | tf_op jit(solution)/shard_map/all_gather | solution.py:123
  438.5 6.2 reshape.168
  446.0 0.7 copy-done.1
  446.7 3.3 convolution_convert_fusion
  450.0 1.0 reshape.156
  451.3 1.0 fusion.54
  453.0 122.6 %all-gather.27.cloned.1.call-done = bf16[64,12,768]{2,1,0:T(8,128)(2,1)} async-done(((bf16[1,12,768]{2,1,0:T(8,128)(2,1)}), bf16[64,12,768]{2,1,0:T(8,128)(2,1)}) %all-gather.27.cloned.1.call-update) | async-done | bytes 1179664 | tf_op jit(solution)/shard_map/all_gather | solution.py:137
  575.6 2.2 reshape.170
  577.8 44.5 %all-gather.17.cloned.1.call-done = bf16[1,4,4,12,64,64]{5,4,3,2,1,0:T(8,128)(2,1)} async-done(((bf16[1,4,4,12,8,64]{5,4,3,2,1,0:T(8,128)(2,1)}), bf16[1,4,4,12,64,64]{5,4,3,2,1,0:T(8,128)(2,1)}) %all-gather.17.cloned.1.call-update) | async-done | bytes 1572880 | tf_op jit(solution)/shard_map/all_gather | solution.py:129
  622.3 4.6 fusion.56
  626.9 37.7 %all-gather.19.cloned.1.call-done = bf16[1,4,4,12,64,64]{5,4,3,2,1,0:T(8,128)(2,1)} async-done(((bf16[1,4,4,12,8,64]{5,4,3,2,1,0:T(8,128)(2,1)}), bf16[1,4,4,12,64,64]{5,4,3,2,1,0:T(8,128)(2,1)}) %all-gather.19.cloned.1.call-update) | async-done | bytes 1572880 | tf_op jit(solution)/shard_map/all_gather | solution.py:130
  664.7 3.1 fusion.24
  669.3 0.8 multiply_convert_fusion
  670.1 33.1 %all-gather.15.cloned.1.call-done = bf16[1024,768]{1,0:T(8,128)(2,1)} async-done(((bf16[128,768]{1,0:T(8,128)(2,1)}), bf16[1024,768]{1,0:T(8,128)(2,1)}) %all-gather.15.cloned.1.call-update) | async-done | bytes 1572880 | tf_op jit(solution)/shard_map/all_gather | solution.py:143
  703.3 4.6 convolution_convert_fusion.2
  707.9 0.7 copy-done.6
  709.2 37.5 %reduce-scatter.2.cloned.1.call-done = bf16[128,768]{1,0:T(8,128)(2,1)} async-done(((bf16[1024,768]{1,0:T(8,128)(2,1)}), bf16[128,768]{1,0:T(8,128)(2,1)}) %reduce-scatter.2.cloned.1.call-update) | async-done | bytes 196624 | tf_op jit(solution)/shard_map/reduce_scatter | solution.py:148
  746.8 1.4 compare_select_fusion
  748.2 0.7 reduce_window_sum.11
  749.1 13.4 %all-gather.2 = f32[32,4,1]{1,2,0:T(1,128)S(1)} all-gather(f32[4,4,1]{1,2,0:T(1,128)S(1)} %copy.138), channel_id=4, replica_groups=mesh['gx'=64,'gz'=8] {'gz'}, dimensions={0}, use_global_device_ids=true | all-gather | bytes 576 | tf_op jit(solution)/shard_map/all_gather | solution.py:13
  762.8 0.7 broadcast_add_fusion
  763.5 1.6 fusion.37
  (136 shorter events, 8.8 us)
Async XLA Ops:
  7.2 696.1 %copy-start = (bf16[384,768]{1,0:T(8,128)(2,1)S(1)}, bf16[384,768]{1,0:T(8,128)(2,1)}, u32[]{:S(2)}) copy-start(bf16[384,768]{1,0:T(8,128)(2,1)} %param.18) | copy-start | bytes 1769476
  7.2 146.5 %all-gather.21.cloned.1.call-start = ((), (), s32[]{:S(2)}) async-start(), calls=%async_computation.9 | async-start | bytes 3993600 | tf_op jit(solution)/shard_map/all_gather | solution.py:91
  7.9 285.6 %all-gather.23.cloned.1.call-start = ((), (), s32[]{:S(2)}) async-start(), calls=%async_computation.10 | async-start | bytes 1597440 | tf_op jit(solution)/shard_map/all_gather | solution.py:117
  8.7 429.8 %all-gather.25.cloned.1.call-start = ((), (), s32[]{:S(2)}) async-start(), calls=%async_computation.11 | async-start | bytes 3993600 | tf_op jit(solution)/shard_map/all_gather | solution.py:123
  16.6 4.4 copy-start.4
  16.6 4.6 copy-start.5
  165.2 11.0 %copy-start.3 = (bf16[1,4,8,12,4,64]{5,3,0,2,4,1:T(8,128)(2,1)S(1)}, bf16[1,4,8,12,4,64]{5,3,0,2,4,1:T(8,128)(2,1)}, u32[]{:S(2)}) copy-start(bf16[1,4,8,12,4,64]{5,3,0,2,4,1:T(8,128)(2,1)} %get-tuple-element.126) | copy-start | bytes 589828
  167.5 25.4 %all-to-all-start.2 = ((bf16[64,2,768]{2,1,0:T(2,128)(2,1)}), bf16[64,2,768]{2,1,0:T(2,128)(2,1)S(1)}, u32[]{:S(2)}, u32[]{:S(2)}) async-start(bf16[64,2,768]{2,1,0:T(2,128)(2,1)} %reshape.176), calls=%async_computation.2 | async-start | bytes 393216 | tf_op jit(solution)/shard_map/all_to_all | solution.py:103
  192.9 21.2 %all-to-all-start.1 = ((bf16[64,2,768]{2,1,0:T(2,128)(2,1)}), bf16[64,2,768]{2,1,0:T(2,128)(2,1)S(1)}, u32[]{:S(2)}, u32[]{:S(2)}) async-start(bf16[64,2,768]{2,1,0:T(2,128)(2,1)} %reshape.180), calls=%async_computation.1 | async-start | bytes 393216 | tf_op jit(solution)/shard_map/all_to_all | solution.py:101
  214.1 21.2 %all-to-all-start = ((bf16[64,2,768]{2,1,0:T(2,128)(2,1)}), bf16[64,2,768]{2,1,0:T(2,128)(2,1)S(1)}, u32[]{:S(2)}, u32[]{:S(2)}) async-start(bf16[64,2,768]{2,1,0:T(2,128)(2,1)} %reshape.178), calls=%async_computation | async-start | bytes 393216 | tf_op jit(solution)/shard_map/all_to_all | solution.py:100
  218.7 356.9 %all-gather.27.cloned.1.call-start = ((), (), s32[]{:S(2)}) async-start(), calls=%async_computation.12 | async-start | bytes 1597440 | tf_op jit(solution)/shard_map/all_gather | solution.py:137
  240.5 204.1 %all-to-all-start.3 = ((bf16[64,2,768]{2,1,0:T(2,128)(2,1)}), bf16[64,2,768]{2,1,0:T(2,128)(2,1)S(1)}, u32[]{:S(2)}, u32[]{:S(2)}) async-start(bf16[64,2,768]{2,1,0:T(2,128)(2,1)} %reshape.182), calls=%async_computation.3 | async-start | bytes 393216 | tf_op jit(solution)/shard_map/all_to_all | solution.py:110
  245.3 377.0 %all-gather.17.cloned.1.call-start = ((), (), s32[]{:S(2)}) async-start(), calls=%async_computation.7 | async-start | bytes 3538944 | tf_op jit(solution)/shard_map/all_gather | solution.py:129
  446.0 0.7 copy-start.1
  452.4 212.3 %all-gather.19.cloned.1.call-start = ((), (), s32[]{:S(2)}) async-start(), calls=%async_computation.8 | async-start | bytes 3538944 | tf_op jit(solution)/shard_map/all_gather | solution.py:130
  452.9 250.3 %all-gather.15.cloned.1.call-start = ((), (), s32[]{:S(2)}) async-start(), calls=%async_computation.5 | async-start | bytes 1769472 | tf_op jit(solution)/shard_map/all_gather | solution.py:143
  667.8 1.0 copy-start.2
  670.1 76.7 %reduce-scatter.2.cloned.1.call-start = ((), (), s32[]{:S(2)}) async-start(), calls=%async_computation.6 | async-start | bytes 1769472 | tf_op jit(solution)/shard_map/reduce_scatter | solution.py:148
  707.9 0.7 copy-start.6
Sparse Core Ops, SparseCore 0:
  11.0 142.6 all-gather.20
  156.6 136.8 all-gather.22
  296.5 141.9 all-gather.24
  441.3 134.2 all-gather.26
  577.5 44.7 all-gather.16
  624.3 40.3 all-gather.18
  670.2 33.0 all-gather.14
  708.1 38.6 reduce-scatter.1
